TPU v7x, 32 devices: a whole 2x2x4 slice. The times are simulated.
32 devices in a mesh: req: 8 (over y, x, core), mdl: 4 (over z).
Axes of the slice: x: 2, y: 2, z: 4, core: 2. Of those that a mesh axis runs over, the one named last changes fastest.
Arguments:
- tokens: bfloat16 [256, 4, 2048], P('req', None, 'mdl'), may hold values from -6 to 6
- counts: int32 [256], P('req'), may hold values from 1 to 4
- new_owner: int32 [256], replicated, may hold values from 0 to 255, as said below
- wkv_state: float32 [256, 32, 4096], P('req', 'mdl'), may hold values from -12 to 12
- att_shift: bfloat16 [256, 2048], P('req', 'mdl'), may hold values from -6 to 6
- ffn_shift: bfloat16 [256, 2048], P('req', 'mdl'), may hold values from -6 to 6
- norm_params: float32 [4, 2048], replicated, may hold values from 0.25 to 1.75
- mix_coeffs: float32 [7, 2048], replicated, may hold values from 0 to 1
- head_params: float32 [7, 2048], P(None, 'mdl'), may hold values from -6 to 2
- recept_weight: bfloat16 [2048, 2048], P(None, 'mdl'), may hold values from -0.125 to 0.125
- key_weight: bfloat16 [2048, 2048], P(None, 'mdl'), may hold values from -0.125 to 0.125
- value_weight: bfloat16 [2048, 2048], P(None, 'mdl'), may hold values from -0.125 to 0.125
- output_weight: bfloat16 [2048, 2048], P('mdl'), may hold values from -0.125 to 0.125
- decay_down: bfloat16 [2048, 96], P('mdl'), may hold values from -0.125 to 0.125
- decay_up: bfloat16 [96, 2048], P(None, 'mdl'), may hold values from -0.625 to 0.625
- alpha_down: bfloat16 [2048, 96], P('mdl'), may hold values from -0.125 to 0.125
- alpha_up: bfloat16 [96, 2048], P(None, 'mdl'), may hold values from -0.625 to 0.625
- gate_down: bfloat16 [2048, 256], P('mdl'), may hold values from -0.125 to 0.125
- gate_up: bfloat16 [256, 2048], P(None, 'mdl'), may hold values from -0.375 to 0.375
- ffn_key_weight: bfloat16 [2048, 4096], P(None, 'mdl'), may hold values from -0.125 to 0.125
- ffn_value_weight: bfloat16 [4096, 2048], P('mdl'), may hold values from -0.09375 to 0.09375
Outputs:
- block_output: bfloat16 [256, 4, 2048], P('req', None, 'mdl')
- new_state: float32 [256, 32, 4096], P('req', 'mdl')
- new_att_shift: bfloat16 [256, 2048], P('req', 'mdl')
- new_ffn_shift: bfloat16 [256, 2048], P('req', 'mdl')
Inputs may be any that keep to these rules, and one draw needn't show every extreme that they name: new_owner is a permutation: the states of request i move to position new_owner[i]. Of the 32 requests of each aligned block of positions, exactly 4 move into each aligned block.
All inputs are finite; a program needn't handle non-finite values.
Results may differ from a plain program's by a relative error of at most 0.0095.
Values may be sent and summed in bfloat16 or wider, within the bound.
No kernel may reach another device: no remote copies, remote signals or barrier semaphores. Data moves between devices by JAX's collectives and lax.ppermute only.
A program may use at most 256 MiB of HBM per device.

v0:
```python
import jax
import jax.numpy as jnp
from jax import lax
from jax.sharding import PartitionSpec as P


def layer_norm(stream, gain_row, offset):
    center = stream - jnp.mean(stream, axis=-1, keepdims=True)
    spread = jnp.mean(center * center, axis=-1, keepdims=True)
    return center / jnp.sqrt(spread + 1e-05) * gain_row + offset


def project(inputs, weight):
    return jnp.dot(inputs, weight, preferred_element_type=jnp.float32)


def split_heads(source, head_size):
    sequence_batch_count, decode_loop_steps_count, feature_count = source.shape
    return source.reshape(
        sequence_batch_count, decode_loop_steps_count, feature_count // head_size, head_size
    )


def advance(wkv_square, decay_now, key_now, value_now, unit_now, alpha_now, recept_now, is_valid):
    removal = -jnp.sum(wkv_square * unit_now[:, :, None, :], axis=-1)
    updated = (
        wkv_square * decay_now[:, :, None, :]
        + removal[..., None] * (unit_now * alpha_now)[:, :, None, :]
        + value_now[..., None] * key_now[:, :, None, :]
    )
    memory_matrix_product = jnp.sum(updated * recept_now[:, :, None, :], axis=-1)
    return (jnp.where(is_valid[:, None, None, None], updated, wkv_square), memory_matrix_product)


def prepare_keys(key_proj, in_context, learned_weights, head_size):
    scaled = split_heads(key_proj * learned_weights[2], head_size)
    key_unit = scaled / jnp.sqrt(jnp.sum(scaled * scaled, axis=-1, keepdims=True) + 1e-06)
    lookup_adjust_factor = key_proj * (1.0 + (in_context - 1.0) * learned_weights[3])
    return (key_unit.reshape(key_proj.shape), lookup_adjust_factor)


def run_heads(
    wkv_flat,
    decay_rate,
    lookup_adjust_factor,
    values,
    key_unit,
    in_context,
    acceptance_matrix_lines,
    live_mask,
    head_size,
):
    sequence_batch_count, decode_loop_steps_count, feature_count = acceptance_matrix_lines.shape
    head_count = feature_count // head_size
    decay_heads = split_heads(decay_rate, head_size)
    keymod_heads = split_heads(lookup_adjust_factor, head_size)
    payload_each_group = split_heads(values, head_size)
    unit_heads = split_heads(key_unit, head_size)
    alpha_heads = split_heads(in_context, head_size)
    recept_heads = split_heads(acceptance_matrix_lines, head_size)
    wkv_square = wkv_flat.reshape(sequence_batch_count, head_count, head_size, head_size)
    readouts = []
    for position in range(decode_loop_steps_count):
        wkv_square, memory_matrix_product = advance(
            wkv_square,
            decay_heads[:, position],
            keymod_heads[:, position],
            payload_each_group[:, position],
            unit_heads[:, position],
            alpha_heads[:, position],
            recept_heads[:, position],
            live_mask[:, position] > 0.5,
        )
        readouts.append(memory_matrix_product)
    stacked = jnp.stack(readouts, axis=1).reshape(
        sequence_batch_count, decode_loop_steps_count, feature_count
    )
    return (stacked, wkv_square.reshape(sequence_batch_count, head_count, head_size * head_size))


def finish_heads(
    memory_matrix_product,
    acceptance_matrix_lines,
    lookup_adjust_factor,
    values,
    sigmoid_scaling_entries,
    learned_weights,
    head_size,
):
    stacked = split_heads(memory_matrix_product, head_size)
    center = stacked - jnp.mean(stacked, axis=-1, keepdims=True)
    spread = jnp.mean(center * center, axis=-1, keepdims=True)
    layernormed_activations = (center / jnp.sqrt(spread + 0.00064)).reshape(
        memory_matrix_product.shape
    ) * learned_weights[5] + learned_weights[6]
    extra_term_share = jnp.sum(
        split_heads(acceptance_matrix_lines * lookup_adjust_factor * learned_weights[4], head_size),
        axis=-1,
        keepdims=True,
    ) * split_heads(values, head_size)
    return (
        (layernormed_activations + extra_term_share.reshape(memory_matrix_product.shape))
        * sigmoid_scaling_entries
    ).astype(jnp.bfloat16)


def per_device(
    tokens,
    counts,
    new_owner,
    wkv_state,
    att_shift,
    ffn_shift,
    norm_params,
    mix_coeffs,
    head_params,
    recept_weight,
    key_weight,
    value_weight,
    output_weight,
    decay_down,
    decay_up,
    alpha_down,
    alpha_up,
    gate_down,
    gate_up,
    ffn_key_weight,
    ffn_value_weight,
):
    groups = lax.axis_size("req")
    sequence_batch_count, decode_loop_steps_count, local_width = tokens.shape
    per_pair = sequence_batch_count // groups
    req_rank = lax.axis_index("req")
    column_start = lax.axis_index("mdl") * local_width
    head_size = local_width // wkv_state.shape[1]
    row_count = sequence_batch_count * decode_loop_steps_count
    shape_three = (sequence_batch_count, decode_loop_steps_count, local_width)
    slot_ids = jnp.arange(decode_loop_steps_count, dtype=jnp.int32)
    live_mask = (slot_ids[None, :] < counts[:, None]).astype(jnp.float32)
    own_block = lax.dynamic_slice_in_dim(
        new_owner, req_rank * sequence_batch_count, sequence_batch_count
    )
    sending = jnp.argsort(own_block)
    sorted_rows = jnp.sort(new_owner.reshape(groups, sequence_batch_count), axis=1)
    arriving = (
        lax.dynamic_slice_in_dim(sorted_rows, req_rank * per_pair, per_pair, 1)
        - req_rank * sequence_batch_count
    )
    placing = jnp.argsort(arriving.reshape(-1))
    sent_state = wkv_state[sending].reshape((groups, per_pair) + wkv_state.shape[1:])
    sent_att = att_shift[sending].astype(jnp.float32).reshape(groups, per_pair, local_width)
    sent_ffn = ffn_shift[sending].astype(jnp.float32).reshape(groups, per_pair, local_width)
    got_state, got_att, got_ffn = (
        lax.all_to_all(sent_state, "req", split_axis=0, concat_axis=0, tiled=True),
        lax.all_to_all(sent_att, "req", split_axis=0, concat_axis=0, tiled=True),
        lax.all_to_all(sent_ffn, "req", split_axis=0, concat_axis=0, tiled=True),
    )
    moved_state = got_state.reshape((sequence_batch_count,) + wkv_state.shape[1:])[placing]
    moved_att = got_att.reshape(sequence_batch_count, local_width)[placing].astype(jnp.bfloat16)
    moved_ffn = got_ffn.reshape(sequence_batch_count, local_width)[placing].astype(jnp.bfloat16)
    full_tokens = lax.all_gather(tokens, "mdl", axis=2, tiled=True)
    full_stream = full_tokens.astype(jnp.float32)
    entire_channel_count = full_tokens.shape[2]
    prev_att, prev_ffn = (
        lax.all_gather(moved_att, "mdl", axis=1, tiled=True),
        lax.all_gather(moved_ffn, "mdl", axis=1, tiled=True),
    )
    normed_one = layer_norm(full_stream, norm_params[0], norm_params[1])
    before_one = jnp.concatenate(
        [prev_att.astype(jnp.float32)[:, None], normed_one[:, :-1]], axis=1
    )
    delta_one = before_one - normed_one
    normed_local = lax.dynamic_slice_in_dim(normed_one, column_start, local_width, 2)

    def mixed_input(mix_index):
        return (
            (normed_one + delta_one * mix_coeffs[mix_index])
            .astype(jnp.bfloat16)
            .reshape(row_count, entire_channel_count)
        )

    decay_full, alpha_full, gate_full = (
        lax.all_gather(decay_down, "mdl", axis=0, tiled=True),
        lax.all_gather(alpha_down, "mdl", axis=0, tiled=True),
        lax.all_gather(gate_down, "mdl", axis=0, tiled=True),
    )
    decay_sum = project(mixed_input(1), decay_full)
    alpha_sum = project(mixed_input(4), alpha_full)
    gate_sum = project(mixed_input(5), gate_full)
    decay_low = jnp.tanh(decay_sum).astype(jnp.bfloat16)
    alpha_low = alpha_sum.astype(jnp.bfloat16)
    gate_low = jax.nn.sigmoid(gate_sum).astype(jnp.bfloat16)
    decay_rate = jnp.exp(
        -0.606531 * jax.nn.sigmoid(head_params[0] + project(decay_low, decay_up))
    ).reshape(shape_three)
    in_context = jax.nn.sigmoid(head_params[1] + project(alpha_low, alpha_up)).reshape(shape_three)
    sigmoid_scaling_entries = project(gate_low, gate_up).reshape(shape_three)
    acceptance_matrix_lines = project(mixed_input(0), recept_weight).reshape(shape_three)
    key_proj = project(mixed_input(2), key_weight).reshape(shape_three)
    values = project(mixed_input(3), value_weight).reshape(shape_three)
    key_unit, lookup_adjust_factor = prepare_keys(key_proj, in_context, head_params, head_size)
    memory_matrix_product, new_state = run_heads(
        moved_state,
        decay_rate,
        lookup_adjust_factor,
        values,
        key_unit,
        in_context,
        acceptance_matrix_lines,
        live_mask,
        head_size,
    )
    attention_group_result = finish_heads(
        memory_matrix_product,
        acceptance_matrix_lines,
        lookup_adjust_factor,
        values,
        sigmoid_scaling_entries,
        head_params,
        head_size,
    )
    attended_term = project(attention_group_result.reshape(row_count, local_width), output_weight)
    attended = lax.psum_scatter(attended_term, "mdl", scatter_dimension=1, tiled=True).reshape(
        shape_three
    )
    midstream = (tokens.astype(jnp.float32) + attended).astype(jnp.bfloat16)
    full_mid = lax.all_gather(midstream, "mdl", axis=2, tiled=True)
    normed_two = layer_norm(full_mid.astype(jnp.float32), norm_params[2], norm_params[3])
    before_two = jnp.concatenate(
        [prev_ffn.astype(jnp.float32)[:, None], normed_two[:, :-1]], axis=1
    )
    ffn_in = (
        (normed_two + (before_two - normed_two) * mix_coeffs[6])
        .astype(jnp.bfloat16)
        .reshape(row_count, entire_channel_count)
    )
    hidden = jnp.square(jax.nn.relu(project(ffn_in, ffn_key_weight))).astype(jnp.bfloat16)
    ffn_out = (
        lax.psum_scatter(
            project(hidden, ffn_value_weight).astype(jnp.bfloat16),
            "mdl",
            scatter_dimension=1,
            tiled=True,
        )
        .astype(jnp.float32)
        .reshape(shape_three)
    )
    block_output = jnp.where(
        live_mask[..., None] > 0.5, midstream.astype(jnp.float32) + ffn_out, 0.0
    ).astype(jnp.bfloat16)
    chosen = (slot_ids[None, :] == (counts - 1)[:, None]).astype(jnp.float32)
    normed_two_local = lax.dynamic_slice_in_dim(normed_two, column_start, local_width, 2)
    new_att_shift = jnp.sum(normed_local * chosen[..., None], axis=1).astype(jnp.bfloat16)
    new_ffn_shift = jnp.sum(normed_two_local * chosen[..., None], axis=1).astype(jnp.bfloat16)
    return (block_output, new_state, new_att_shift, new_ffn_shift)


def solution(mesh):
    return jax.shard_map(
        per_device,
        mesh=mesh,
        in_specs=(
            P("req", None, "mdl"),
            P("req"),
            P(),
            P("req", "mdl", None),
            P("req", "mdl"),
            P("req", "mdl"),
            P(),
            P(),
            P(None, "mdl"),
            P(None, "mdl"),
            P(None, "mdl"),
            P(None, "mdl"),
            P("mdl", None),
            P("mdl", None),
            P(None, "mdl"),
            P("mdl", None),
            P(None, "mdl"),
            P("mdl", None),
            P(None, "mdl"),
            P(None, "mdl"),
            P("mdl", None),
        ),
        out_specs=(P("req", None, "mdl"), P("req", "mdl", None), P("req", "mdl"), P("req", "mdl")),
        check_vma=False,
    )
```

profile of v0, /device:TPU:0, one launch (start us, length us, event | category | flops | bytes accessed | tf_op | source)
XLA Modules:
  0.0 439.1 jit_solution(6680961267923316029)
XLA Ops:
  27.7 20.2 %all_gather.23 = bf16[2048,96]{0,1:T(8,128)(2,1)} all-gather(bf16[512,96]{0,1:T(8,128)(2,1)} %param.34), channel_id=1, replica_groups=mesh['req'=8,'mdl'=4] {'mdl'}, dimensions={0}, use_global_device_ids=true | all-gather | bytes 491520 | tf_op jit(solution)/shard_map/all_gather | solution.py:183
  47.9 15.2 %all_gather.24 = bf16[2048,96]{0,1:T(8,128)(2,1)S(1)} all-gather(bf16[512,96]{0,1:T(8,128)(2,1)} %param.36), channel_id=1, replica_groups=mesh['req'=8,'mdl'=4] {'mdl'}, dimensions={0}, use_global_device_ids=true | all-gather | bytes 491520 | tf_op jit(solution)/shard_map/all_gather | solution.py:184
  63.2 14.9 %all_gather.21 = bf16[32,4,2048]{2,1,0:T(4,128)(2,1)S(1)} all-gather(bf16[32,4,512]{2,1,0:T(4,128)(2,1)} %param.21), channel_id=1, replica_groups=mesh['req'=8,'mdl'=4] {'mdl'}, dimensions={2}, use_global_device_ids=true | all-gather | bytes 655360 | tf_op jit(solution)/shard_map/all_gather | solution.py:161
  94.9 13.7 %all_gather.22 = bf16[32,2048]{1,0:T(8,128)(2,1)S(1)} all-gather(bf16[32,512]{1,0:T(8,128)(2,1)S(1)} %gather_fusion.3), channel_id=1, replica_groups=mesh['req'=8,'mdl'=4] {'mdl'}, dimensions={1}, use_global_device_ids=true | all-gather | bytes 163840 | tf_op jit(solution)/shard_map/all_gather | solution.py:165
  162.2 8.3 %reshape.338 = f32[32,8,64,64]{3,2,1,0:T(8,128)} reshape(f32[32,8,4096]{2,1,0:T(8,128)} %gather_fusion.1) | data formatting | bytes 8388608 | tf_op jit(solution)/shard_map/reshape | solution.py:61
  176.4 11.0 %multiply_reduce_fusion.6 = (f32[32,8,64]{2,1,0:T(8,128)S(1)}, f32[32,8,64]{2,1,0:T(8,128)S(1)}) fusion(f32[32,8,64]{2,1,0:T(8,128)S(1)} %copy-done.8, f32[32,8,64,64]{3,2,1,0:T(8,128)S(1)} %copy-done.2, f32[32,8,64]{2,1,0:T(8,128)S(1)} %get-tuple-element.51, f32[32,8,64]{2,1,0:T(8,128)S(1)} %get-tuple-element.30, f32[32,8,64]{2,1,0:T(8,128)S(1)} %neg.38, ...), kind=kLoop, calls=%fused_computation.14 | loop fusion | flops 10452992 | bytes 4784160 | tf_op jit(solution)/shard_map/reduce_sum | solution.py:31
  188.8 18.7 %multiply_reduce_fusion.3 = (f32[32,8,64]{2,1,0:T(8,128)S(1)}, f32[32,8,64,64]{3,2,1,0:T(8,128)}, f32[32,8,64]{2,1,0:T(8,128)S(1)}, f32[32,8,64,64]{3,2,1,0:T(8,...) fusion(f32[32,8,64]{2,1,0:T(8,128)} %get-tuple-element.92, ...), kind=kLoop, calls=%fused_computation.10 | loop fusion | flops 16744448 | bytes 26083392 | tf_op jit(solution)/shard_map/reduce_sum | solution.py:25
  208.3 12.5 %multiply_reduce_fusion.2 = (f32[32,8,64]{2,1,0:T(8,128)S(1)}, f32[32,8,64]{2,1,0:T(8,128)S(1)}, f32[32,8,64,64]{3,2,1,0:T(8,128)}, f32[32,8,64,64]{3,2,1,0:T(8,128)}) fusion(f32[32,8,64]{2,1,0:T(8,128)} %get-tuple-element.34, f32[32,8,64,64]{3,2,1,0:T(8,128)} %get-tuple-element.18, f32[32,8,64]{2,1,0:T(8,128)S(1)} %get-tuple-element.48, ...), kind=kLoop, calls=%fused_computation.8 | loop fusion | flops 10452992 | bytes 13172768 | tf_op jit(solution)/shard_map/reduce_sum | solution.py:31
  222.2 15.5 %broadcast_multiply_fusion.1 = (f32[32,8,64,64]{3,2,1,0:T(8,128)}, f32[32,8,64]{2,1,0:T(8,128)S(1)}, f32[32,8,64,64]{3,2,1,0:T(8,128)}) fusion(f32[32,8,64]{2,1,0:T(8,128)} %get-tuple-element.31, f32[32,8,64]{2,1,0:T(8,128)} %neg.42, f32[32,8,64]{2,1,0:T(8,128)} %get-tuple-element.33, f32[32,8,64]{2,1,0:T(8,128)} %get-tuple-element.40, ...), kind=kLoop, calls=%fused_computation.19 | loop fusion | flops 13615104 | bytes 13369376 | tf_op jit(solution)/shard_map/mul | solution.py:28
  256.3 14.6 %all_gather.27 = bf16[32,2048]{1,0:T(8,128)(2,1)S(1)} all-gather(bf16[32,512]{1,0:T(8,128)(2,1)S(1)} %gather_fusion.5), channel_id=1, replica_groups=mesh['req'=8,'mdl'=4] {'mdl'}, dimensions={1}, use_global_device_ids=true | all-gather | bytes 163840 | tf_op jit(solution)/shard_map/all_gather | solution.py:166
  274.9 8.1 %mul.647 = f32[32,8,4096]{2,1,0:T(8,128)} reshape(f32[32,8,64,64]{3,2,1,0:T(8,128)} %mul.597) | data formatting | bytes 8388608 | tf_op jit(solution)/shard_map/mul | solution.py:27
  286.7 7.9 %mul.639 = f32[32,8,4096]{2,1,0:T(8,128)} reshape(f32[32,8,64,64]{3,2,1,0:T(8,128)} %mul.561) | data formatting | bytes 8388608 | tf_op jit(solution)/shard_map/mul | solution.py:27
  298.3 7.9 %mul.643 = f32[32,8,4096]{2,1,0:T(8,128)} reshape(f32[32,8,64,64]{3,2,1,0:T(8,128)} %mul.579) | data formatting | bytes 8388608 | tf_op jit(solution)/shard_map/mul | solution.py:27
  309.9 7.9 %mul.635 = f32[32,8,4096]{2,1,0:T(8,128)} reshape(f32[32,8,64,64]{3,2,1,0:T(8,128)} %mul.523) | data formatting | bytes 8388608 | tf_op jit(solution)/shard_map/mul | solution.py:27
  317.8 7.9 %mul.637 = f32[32,8,4096]{2,1,0:T(8,128)} reshape(f32[32,8,64,64]{3,2,1,0:T(8,128)} %get-tuple-element.52) | data formatting | bytes 8388608 | tf_op jit(solution)/shard_map/mul | solution.py:28
  325.7 7.9 %mul.638 = f32[32,8,4096]{2,1,0:T(8,128)} reshape(f32[32,8,64,64]{3,2,1,0:T(8,128)} %get-tuple-element.53) | data formatting | bytes 8388608 | tf_op jit(solution)/shard_map/mul | solution.py:29
  333.6 7.9 %mul.641 = f32[32,8,4096]{2,1,0:T(8,128)} reshape(f32[32,8,64,64]{3,2,1,0:T(8,128)} %get-tuple-element.54) | data formatting | bytes 8388608 | tf_op jit(solution)/shard_map/mul | solution.py:28
  341.5 7.9 %mul.642 = f32[32,8,4096]{2,1,0:T(8,128)} reshape(f32[32,8,64,64]{3,2,1,0:T(8,128)} %get-tuple-element.55) | data formatting | bytes 8388608 | tf_op jit(solution)/shard_map/mul | solution.py:29
  349.4 7.9 %mul.645 = f32[32,8,4096]{2,1,0:T(8,128)} reshape(f32[32,8,64,64]{3,2,1,0:T(8,128)} %get-tuple-element.56) | data formatting | bytes 8388608 | tf_op jit(solution)/shard_map/mul | solution.py:28
  357.3 7.9 %mul.646 = f32[32,8,4096]{2,1,0:T(8,128)} reshape(f32[32,8,64,64]{3,2,1,0:T(8,128)} %get-tuple-element.57) | data formatting | bytes 8388608 | tf_op jit(solution)/shard_map/mul | solution.py:29
  365.2 7.9 %mul.649 = f32[32,8,4096]{2,1,0:T(8,128)} reshape(f32[32,8,64,64]{3,2,1,0:T(8,128)} %get-tuple-element.58) | data formatting | bytes 8388608 | tf_op jit(solution)/shard_map/mul | solution.py:28
  373.1 7.9 %mul.650 = f32[32,8,4096]{2,1,0:T(8,128)} reshape(f32[32,8,64,64]{3,2,1,0:T(8,128)} %get-tuple-element.60) | data formatting | bytes 8388608 | tf_op jit(solution)/shard_map/mul | solution.py:29
  382.2 16.0 %all_gather.26 = bf16[32,4,2048]{2,1,0:T(4,128)(2,1)S(1)} all-gather(bf16[32,4,512]{2,1,0:T(4,128)(2,1)S(1)} %add_convert_fusion.6), channel_id=1, replica_groups=mesh['req'=8,'mdl'=4] {'mdl'}, dimensions={2}, use_global_device_ids=true | all-gather | bytes 655360 | tf_op jit(solution)/shard_map/all_gather | solution.py:227
  406.3 22.3 %add_select_fusion = f32[32,8,4096]{2,1,0:T(8,128)} fusion(f32[32,8,4096]{2,1,0:T(8,128)} %mul.650, f32[32,8,4096]{2,1,0:T(8,128)} %mul.649, f32[32,8,4096]{2,1,0:T(8,128)} %mul.647, f32[32,8,4096]{2,1,0:T(8,128)} %mul.646, f32[32,8,4096]{2,1,0:T(8,128)} %mul.645, f32[32,8,4096]{2,1,0:T(8,128)} %mul.643, f32[32,8,4096]{2,1,0:T(8,128)} %mul.642, ...), kind=kLoop, calls=%fused_computation.17 | loop fusion | flops 16777216 | bytes 58720384 | tf_op jit(solution)/shard_map/jit(_where)/select_n | solution.py:32
  (186 shorter events, 146.7 us)
Async XLA Ops:
  7.2 234.8 %copy-start = (bf16[512,2048]{1,0:T(8,128)(2,1)S(1)}, bf16[512,2048]{1,0:T(8,128)(2,1)}, u32[]{:S(2)}) copy-start(bf16[512,2048]{1,0:T(8,128)(2,1)} %param.33) | copy-start | bytes 6291460
  7.2 147.5 %all-gather.2.cloned.1.call-start = ((), (), s32[]{:S(2)}) async-start(), calls=%async_computation.5 | async-start | bytes 1310720 | tf_op jit(solution)/shard_map/all_gather | solution.py:185
  10.3 79.1 %copy-start.20 = (s32[1024]{0:T(1024)}, s32[1024]{0:T(1024)S(1)}, u32[]{:S(2)}) copy-start(s32[1024]{0:T(1024)S(1)} %pad_clamp_fusion.1) | copy-start | bytes 12292
  12.3 77.0 %all-to-all-start.1 = ((bf16[8,4,512]{2,1,0:T(4,128)(2,1)}), bf16[8,4,512]{2,1,0:T(4,128)(2,1)S(1)}, u32[]{:S(2)}, u32[]{:S(2)}) async-start(bf16[8,4,512]{2,1,0:T(4,128)(2,1)} %reshape.354), calls=%async_computation.1 | async-start | bytes 65536 | tf_op jit(solution)/shard_map/all_to_all | solution.py:155
  25.9 63.5 %copy-start.11 = (f32[1,2048]{1,0:T(1,128)}, f32[1,2048]{1,0:T(1,128)S(1)}, u32[]{:S(2)}) copy-start(f32[1,2048]{1,0:T(1,128)S(1)} %get-tuple-element.70) | copy-start | bytes 24580
  25.9 63.5 %copy-start.12 = (f32[1,2048]{1,0:T(1,128)}, f32[1,2048]{1,0:T(1,128)S(1)}, u32[]{:S(2)}) copy-start(f32[1,2048]{1,0:T(1,128)S(1)} %get-tuple-element.71) | copy-start | bytes 24580
  89.4 67.7 %all-to-all-start = ((f32[8,4,8,4096]{3,2,1,0:T(8,128)}), f32[8,4,8,4096]{3,2,1,0:T(8,128)}, u32[]{:S(2)}, u32[]{:S(2)}) async-start(f32[8,4,8,4096]{3,2,1,0:T(8,128)} %bitcast.175), calls=%async_computation | async-start | bytes 8388608 | tf_op jit(solution)/shard_map/all_to_all | solution.py:154
  94.2 286.9 %reduce-scatter.3.cloned.1.call-start = ((), (), s32[]{:S(2)}) async-start(), calls=%async_computation.6 | async-start | bytes 1310720 | tf_op jit(solution)/shard_map/reduce_scatter | solution.py:223
  162.2 14.1 %copy-start.5 = (f32[32,8,64]{2,1,0:T(8,128)S(1)}, f32[32,8,64]{2,1,0:T(8,128)}, u32[]{:S(2)}) copy-start(f32[32,8,64]{2,1,0:T(8,128)} %copy.91) | copy-start | bytes 196612
  162.2 14.1 %copy-start.19 = (pred[32]{0:T(512)(128)(4,1)S(1)}, pred[32]{0:T(512)(128)(4,1)}, u32[]{:S(2)}) copy-start(pred[32]{0:T(512)(128)(4,1)} %get-tuple-element.83) | copy-start | bytes 100
  170.5 18.2 %copy-start.22 = (pred[32]{0:T(512)(128)(4,1)S(1)}, pred[32]{0:T(512)(128)(4,1)}, u32[]{:S(2)}) copy-start(pred[32]{0:T(512)(128)(4,1)} %get-tuple-element.82) | copy-start | bytes 100
  188.7 19.5 %copy-start.4 = (f32[32,8,64]{2,1,0:T(8,128)S(1)}, f32[32,8,64]{2,1,0:T(8,128)}, u32[]{:S(2)}) copy-start(f32[32,8,64]{2,1,0:T(8,128)} %copy.96) | copy-start | bytes 196612
  188.7 19.5 %copy-start.18 = (pred[32]{0:T(512)(128)(4,1)S(1)}, pred[32]{0:T(512)(128)(4,1)}, u32[]{:S(2)}) copy-start(pred[32]{0:T(512)(128)(4,1)} %get-tuple-element.81) | copy-start | bytes 100
  208.3 13.9 %copy-start.7 = (f32[32,8,64]{2,1,0:T(8,128)S(1)}, f32[32,8,64]{2,1,0:T(8,128)}, u32[]{:S(2)}) copy-start(f32[32,8,64]{2,1,0:T(8,128)} %get-tuple-element.49) | copy-start | bytes 196612
  222.2 19.8 %copy-start.16 = (f32[1,512]{1,0:T(1,128)S(1)}, f32[1,512]{1,0:T(1,128)}, u32[]{:S(2)}) copy-start(f32[1,512]{1,0:T(1,128)} %get-tuple-element.73) | copy-start | bytes 6148
  222.2 19.8 %copy-start.17 = (f32[1,512]{1,0:T(1,128)S(1)}, f32[1,512]{1,0:T(1,128)}, u32[]{:S(2)}) copy-start(f32[1,512]{1,0:T(1,128)} %get-tuple-element.79) | copy-start | bytes 6148
  246.2 9.4 %all-to-all-start.2 = ((bf16[8,4,512]{2,1,0:T(4,128)(2,1)}), bf16[8,4,512]{2,1,0:T(4,128)(2,1)S(1)}, u32[]{:S(2)}, u32[]{:S(2)}) async-start(bf16[8,4,512]{2,1,0:T(4,128)(2,1)} %reshape.356), calls=%async_computation.3 | async-start | bytes 65536 | tf_op jit(solution)/shard_map/all_to_all | solution.py:156
  250.7 179.8 %reduce-scatter.5.cloned.1.call-start = ((), (), s32[]{:S(2)}) async-start(), calls=%async_computation.7 | async-start | bytes 655360 | tf_op jit(solution)/shard_map/reduce_scatter | solution.py:239
  373.1 25.9 %copy-start.13 = (f32[1,2048]{1,0:T(1,128)S(1)}, f32[1,2048]{1,0:T(1,128)}, u32[]{:S(2)}) copy-start(f32[1,2048]{1,0:T(1,128)} %get-tuple-element.69) | copy-start | bytes 24580
  373.1 25.9 %copy-start.14 = (f32[1,2048]{1,0:T(1,128)S(1)}, f32[1,2048]{1,0:T(1,128)}, u32[]{:S(2)}) copy-start(f32[1,2048]{1,0:T(1,128)} %get-tuple-element.72) | copy-start | bytes 24580
  373.1 26.3 %copy-start.15 = (f32[1,2048]{1,0:T(1,128)S(1)}, f32[1,2048]{1,0:T(1,128)}, u32[]{:S(2)}) copy-start(f32[1,2048]{1,0:T(1,128)} %get-tuple-element.62) | copy-start | bytes 24580
  382.2 24.1 %copy-start.23 = (pred[32]{0:T(512)(128)(4,1)S(1)}, pred[32]{0:T(512)(128)(4,1)}, u32[]{:S(2)}) copy-start(pred[32]{0:T(512)(128)(4,1)} %get-tuple-element.82) | copy-start | bytes 100
  382.2 24.1 %copy-start.25 = (pred[32]{0:T(512)(128)(4,1)S(1)}, pred[32]{0:T(512)(128)(4,1)}, u32[]{:S(2)}) copy-start(pred[32]{0:T(512)(128)(4,1)} %get-tuple-element.80) | copy-start | bytes 100
  406.3 26.0 %copy-start.1 = (bf16[512,2048]{1,0:T(8,128)(2,1)S(1)}, bf16[512,2048]{1,0:T(8,128)(2,1)}, u32[]{:S(2)}) copy-start(bf16[512,2048]{1,0:T(8,128)(2,1)} %param.33) | copy-start | bytes 6291460
  (9 other events, 86.3 us)
Sparse Core Ops, SparseCore 0:
  9.6 36.9 all-gather.1
  244.9 30.9 reduce-scatter.2
  406.4 20.1 reduce-scatter.4
where the time goes:
time: 445 us; the launch traced here: 439 us
  local copies, waits for them, and re-layouts  175 us (39%)
  other arithmetic  112 us (25%)
  blocking collectives  94.6 us (21%)
  matrix products  23 us (5%)
  starting transfers between devices  14.6 us (3%)
  between operations  14.5 us (3%)
  waiting for transfers between devices  5.32 us (1%)
    mul x9, local copies, waits for them, and re-layouts, advance(): wkv_square * decay_now[:, :, None, :]  48.5 us
    mul x10, local copies, waits for them, and re-layouts, advance(): value_now[..., None] * key_now[:, :, None, :]  37.6 us
    mul x4, local copies, waits for them, and re-layouts, advance(): removal[..., None] * (unit_now * alpha_now)[:, :, None, :]  31.6 us
    reduce_sum x2, other arithmetic, advance(): removal = -jnp.sum(wkv_square * unit_now[:, :, None, :], axis=-1)  24.5 us
    reduce_sum x2, other arithmetic, advance(): jnp.sum(updated * recept_now[:, :, None, :], axis=-1)  23.4 us
    dot_general x8, matrix products, project(): return jnp.dot(inputs, weight, preferred_element_type=jnp.float32)  23 us
    select_n x1, other arithmetic, advance(): jnp.where(is_valid[:, None, None, None], updated, wkv_square)  22.3 us
    all_gather x1, blocking collectives, per_device(): lax.all_gather(decay_down, 'mdl', axis=0, tiled=True)  20.2 us
  transfers between devices with their start and end apart: 6, of which 1 were waited for; matrix products, arithmetic and copies ran while one was open for 48% of the time, Pallas kernels for 0%

commit v1 on v0

--- a/solution.py
+++ b/solution.py
@@ -127,6 +127,19 @@
     ffn_key_weight,
     ffn_value_weight,
 ):
+
+    def meet_slabs(block_here, a_name):
+        world_n = lax.axis_size(a_name)
+        block_now = block_here
+        block_list = [block_now]
+        block_next = [(dev_j - 1, dev_j) for dev_j in range(1, world_n)] + [(world_n - 1, 0)]
+        for _ in range(world_n - 1):
+            block_now = lax.ppermute(block_now, a_name, block_next)
+            block_list += [block_now]
+        new = jnp.concatenate([*reversed(block_list)], axis=2)
+        step_out = jnp.roll(new, (lax.axis_index(a_name) + 1) * block_now.shape[2], axis=2)
+        return step_out
+
     groups = lax.axis_size("req")
     sequence_batch_count, decode_loop_steps_count, local_width = tokens.shape
     per_pair = sequence_batch_count // groups
@@ -158,7 +171,7 @@
     moved_state = got_state.reshape((sequence_batch_count,) + wkv_state.shape[1:])[placing]
     moved_att = got_att.reshape(sequence_batch_count, local_width)[placing].astype(jnp.bfloat16)
     moved_ffn = got_ffn.reshape(sequence_batch_count, local_width)[placing].astype(jnp.bfloat16)
-    full_tokens = lax.all_gather(tokens, "mdl", axis=2, tiled=True)
+    full_tokens = meet_slabs(tokens, a_name="mdl")
     full_stream = full_tokens.astype(jnp.float32)
     entire_channel_count = full_tokens.shape[2]
     prev_att, prev_ffn = (

time: 445 us -> 438 us (0.984)
  blocking collectives: 94.6 us -> 78.8 us
  waiting for transfers between devices: 5.32 us -> 10.9 us
    all_gather x1 -> x0, blocking collectives: 14.9 us -> none  [per_device(): full_tokens = lax.all_gather(tokens, 'mdl', axis=2, tiled=True)]
    ppermute x0 -> x3, waiting for transfers between devices: none -> 5.54 us  [meet_slabs(): block_now = lax.ppermute(block_now, a_name, block_next)]
  transfers between devices with their start and end apart: 6 -> 9, of which waited for: 1 -> 2; matrix products, arithmetic and copies ran while one was open for 48% -> 49% of each run, Pallas kernels for 0% -> 0%
where the time goes in v1:
time: 438 us; the launch traced here: 431 us
  local copies, waits for them, and re-layouts  178 us (41%)
  other arithmetic  108 us (25%)
  blocking collectives  78.8 us (18%)
  matrix products  23.9 us (5%)
  starting transfers between devices  17.2 us (4%)
  between operations  14.5 us (3%)
  waiting for transfers between devices  10.9 us (2%)
    mul x9, local copies, waits for them, and re-layouts, advance(): wkv_square * decay_now[:, :, None, :]  48.5 us
    mul x10, local copies, waits for them, and re-layouts, advance(): value_now[..., None] * key_now[:, :, None, :]  37.6 us
    mul x4, local copies, waits for them, and re-layouts, advance(): removal[..., None] * (unit_now * alpha_now)[:, :, None, :]  31.6 us
    reduce_sum x2, other arithmetic, advance(): removal = -jnp.sum(wkv_square * unit_now[:, :, None, :], axis=-1)  25.3 us
    dot_general x8, matrix products, project(): return jnp.dot(inputs, weight, preferred_element_type=jnp.float32)  23.9 us
    reduce_sum x2, other arithmetic, advance(): jnp.sum(updated * recept_now[:, :, None, :], axis=-1)  23.7 us
    select_n x1, other arithmetic, advance(): jnp.where(is_valid[:, None, None, None], updated, wkv_square)  22.3 us
    all_gather x1, blocking collectives, per_device(): lax.all_gather(decay_down, 'mdl', axis=0, tiled=True)  19.2 us
  transfers between devices with their start and end apart: 9, of which 2 were waited for; matrix products, arithmetic and copies ran while one was open for 49% of the time, Pallas kernels for 0%

profile of v1, /device:TPU:0, one launch (start us, length us, event | category | flops | bytes accessed | tf_op | source)
XLA Modules:
  0.0 431.0 jit_solution(2686062267503015110)
XLA Ops:
  28.6 19.2 %all_gather.19 = bf16[2048,96]{0,1:T(8,128)(2,1)} all-gather(bf16[512,96]{0,1:T(8,128)(2,1)} %param.34), channel_id=1, replica_groups=mesh['req'=8,'mdl'=4] {'mdl'}, dimensions={0}, use_global_device_ids=true | all-gather | bytes 491520 | tf_op jit(solution)/shard_map/all_gather | solution.py:196
  47.7 16.1 %all_gather.20 = bf16[2048,96]{0,1:T(8,128)(2,1)} all-gather(bf16[512,96]{0,1:T(8,128)(2,1)} %param.36), channel_id=1, replica_groups=mesh['req'=8,'mdl'=4] {'mdl'}, dimensions={0}, use_global_device_ids=true | all-gather | bytes 491520 | tf_op jit(solution)/shard_map/all_gather | solution.py:197
  78.9 13.6 %all_gather.18 = bf16[32,2048]{1,0:T(8,128)(2,1)S(1)} all-gather(bf16[32,512]{1,0:T(8,128)(2,1)S(1)} %gather_fusion.3), channel_id=1, replica_groups=mesh['req'=8,'mdl'=4] {'mdl'}, dimensions={1}, use_global_device_ids=true | all-gather | bytes 163840 | tf_op jit(solution)/shard_map/all_gather | solution.py:178
  154.5 7.9 %reshape.338 = f32[32,8,64,64]{3,2,1,0:T(8,128)} reshape(f32[32,8,4096]{2,1,0:T(8,128)} %gather_fusion.1) | data formatting | bytes 8388608 | tf_op jit(solution)/shard_map/reshape | solution.py:61
  162.3 5.8 %multiply_reduce_fusion.7 = f32[32,8,64]{2,1,0:T(8,128)S(1)} fusion(f32[32,8,64,64]{3,2,1,0:T(8,128)} %reshape.338, f32[32,8,64]{2,1,0:T(8,128)S(1)} %get-tuple-element.90), kind=kLoop, calls=%fused_computation.16 | loop fusion | flops 2080768 | bytes 4325376 | tf_op jit(solution)/shard_map/reduce_sum | solution.py:25
  168.2 11.0 %multiply_reduce_fusion.6 = (f32[32,8,64]{2,1,0:T(8,128)S(1)}, f32[32,8,64]{2,1,0:T(8,128)S(1)}) fusion(f32[32,8,64]{2,1,0:T(8,128)S(1)} %copy-done.11, f32[32,8,64,64]{3,2,1,0:T(8,128)S(1)} %copy-done.2, f32[32,8,64]{2,1,0:T(8,128)S(1)} %get-tuple-element.51, f32[32,8,64]{2,1,0:T(8,128)S(1)} %get-tuple-element.30, f32[32,8,64]{2,1,0:T(8,128)S(1)} %neg.38, ...), kind=kLoop, calls=%fused_computation.14 | loop fusion | flops 10452992 | bytes 4784160 | tf_op jit(solution)/shard_map/reduce_sum | solution.py:31
  180.5 19.5 %multiply_reduce_fusion.3 = (f32[32,8,64]{2,1,0:T(8,128)S(1)}, f32[32,8,64,64]{3,2,1,0:T(8,128)}, f32[32,8,64]{2,1,0:T(8,128)S(1)}, f32[32,8,64,64]{3,2,1,0:T(8,...) fusion(f32[32,8,64]{2,1,0:T(8,128)} %get-tuple-element.92, ...), kind=kLoop, calls=%fused_computation.10 | loop fusion | flops 16744448 | bytes 26083392 | tf_op jit(solution)/shard_map/reduce_sum | solution.py:25
  200.8 12.8 %multiply_reduce_fusion.2 = (f32[32,8,64]{2,1,0:T(8,128)S(1)}, f32[32,8,64]{2,1,0:T(8,128)S(1)}, f32[32,8,64,64]{3,2,1,0:T(8,128)}, f32[32,8,64,64]{3,2,1,0:T(8,128)}) fusion(f32[32,8,64]{2,1,0:T(8,128)} %get-tuple-element.34, f32[32,8,64,64]{3,2,1,0:T(8,128)} %get-tuple-element.18, f32[32,8,64]{2,1,0:T(8,128)S(1)} %get-tuple-element.48, ...), kind=kLoop, calls=%fused_computation.8 | loop fusion | flops 10452992 | bytes 13172768 | tf_op jit(solution)/shard_map/reduce_sum | solution.py:31
  215.0 15.7 %broadcast_multiply_fusion.1 = (f32[32,8,64,64]{3,2,1,0:T(8,128)}, f32[32,8,64]{2,1,0:T(8,128)S(1)}, f32[32,8,64,64]{3,2,1,0:T(8,128)}) fusion(f32[32,8,64]{2,1,0:T(8,128)} %get-tuple-element.31, f32[32,8,64]{2,1,0:T(8,128)} %neg.42, f32[32,8,64]{2,1,0:T(8,128)} %get-tuple-element.33, f32[32,8,64]{2,1,0:T(8,128)} %get-tuple-element.40, ...), kind=kLoop, calls=%fused_computation.19 | loop fusion | flops 13615104 | bytes 13369376 | tf_op jit(solution)/shard_map/mul | solution.py:28
  248.9 14.9 %all_gather.23 = bf16[32,2048]{1,0:T(8,128)(2,1)S(1)} all-gather(bf16[32,512]{1,0:T(8,128)(2,1)S(1)} %gather_fusion.5), channel_id=1, replica_groups=mesh['req'=8,'mdl'=4] {'mdl'}, dimensions={1}, use_global_device_ids=true | all-gather | bytes 163840 | tf_op jit(solution)/shard_map/all_gather | solution.py:179
  267.8 8.1 %mul.651 = f32[32,8,4096]{2,1,0:T(8,128)} reshape(f32[32,8,64,64]{3,2,1,0:T(8,128)} %mul.601) | data formatting | bytes 8388608 | tf_op jit(solution)/shard_map/mul | solution.py:27
  279.6 7.9 %mul.643 = f32[32,8,4096]{2,1,0:T(8,128)} reshape(f32[32,8,64,64]{3,2,1,0:T(8,128)} %mul.565) | data formatting | bytes 8388608 | tf_op jit(solution)/shard_map/mul | solution.py:27
  291.2 7.9 %mul.647 = f32[32,8,4096]{2,1,0:T(8,128)} reshape(f32[32,8,64,64]{3,2,1,0:T(8,128)} %mul.583) | data formatting | bytes 8388608 | tf_op jit(solution)/shard_map/mul | solution.py:27
  302.9 7.9 %mul.639 = f32[32,8,4096]{2,1,0:T(8,128)} reshape(f32[32,8,64,64]{3,2,1,0:T(8,128)} %mul.527) | data formatting | bytes 8388608 | tf_op jit(solution)/shard_map/mul | solution.py:27
  310.7 7.9 %mul.641 = f32[32,8,4096]{2,1,0:T(8,128)} reshape(f32[32,8,64,64]{3,2,1,0:T(8,128)} %get-tuple-element.52) | data formatting | bytes 8388608 | tf_op jit(solution)/shard_map/mul | solution.py:28
  318.6 7.9 %mul.642 = f32[32,8,4096]{2,1,0:T(8,128)} reshape(f32[32,8,64,64]{3,2,1,0:T(8,128)} %get-tuple-element.53) | data formatting | bytes 8388608 | tf_op jit(solution)/shard_map/mul | solution.py:29
  326.5 7.9 %mul.645 = f32[32,8,4096]{2,1,0:T(8,128)} reshape(f32[32,8,64,64]{3,2,1,0:T(8,128)} %get-tuple-element.54) | data formatting | bytes 8388608 | tf_op jit(solution)/shard_map/mul | solution.py:28
  334.4 7.9 %mul.646 = f32[32,8,4096]{2,1,0:T(8,128)} reshape(f32[32,8,64,64]{3,2,1,0:T(8,128)} %get-tuple-element.55) | data formatting | bytes 8388608 | tf_op jit(solution)/shard_map/mul | solution.py:29
  342.3 7.9 %mul.649 = f32[32,8,4096]{2,1,0:T(8,128)} reshape(f32[32,8,64,64]{3,2,1,0:T(8,128)} %get-tuple-element.56) | data formatting | bytes 8388608 | tf_op jit(solution)/shard_map/mul | solution.py:28
  350.2 7.9 %mul.650 = f32[32,8,4096]{2,1,0:T(8,128)} reshape(f32[32,8,64,64]{3,2,1,0:T(8,128)} %get-tuple-element.57) | data formatting | bytes 8388608 | tf_op jit(solution)/shard_map/mul | solution.py:29
  358.1 7.9 %mul.653 = f32[32,8,4096]{2,1,0:T(8,128)} reshape(f32[32,8,64,64]{3,2,1,0:T(8,128)} %get-tuple-element.58) | data formatting | bytes 8388608 | tf_op jit(solution)/shard_map/mul | solution.py:28
  366.0 7.9 %mul.654 = f32[32,8,4096]{2,1,0:T(8,128)} reshape(f32[32,8,64,64]{3,2,1,0:T(8,128)} %get-tuple-element.60) | data formatting | bytes 8388608 | tf_op jit(solution)/shard_map/mul | solution.py:29
  375.1 15.0 %all_gather.22 = bf16[32,4,2048]{2,1,0:T(4,128)(2,1)S(1)} all-gather(bf16[32,4,512]{2,1,0:T(4,128)(2,1)S(1)} %add_convert_fusion.6), channel_id=1, replica_groups=mesh['req'=8,'mdl'=4] {'mdl'}, dimensions={2}, use_global_device_ids=true | all-gather | bytes 655360 | tf_op jit(solution)/shard_map/all_gather | solution.py:240
  398.2 22.3 %add_select_fusion = f32[32,8,4096]{2,1,0:T(8,128)} fusion(f32[32,8,4096]{2,1,0:T(8,128)} %mul.654, f32[32,8,4096]{2,1,0:T(8,128)} %mul.653, f32[32,8,4096]{2,1,0:T(8,128)} %mul.651, f32[32,8,4096]{2,1,0:T(8,128)} %mul.650, f32[32,8,4096]{2,1,0:T(8,128)} %mul.649, f32[32,8,4096]{2,1,0:T(8,128)} %mul.647, f32[32,8,4096]{2,1,0:T(8,128)} %mul.646, ...), kind=kLoop, calls=%fused_computation.17 | loop fusion | flops 16777216 | bytes 58720384 | tf_op jit(solution)/shard_map/jit(_where)/select_n | solution.py:32
  (190 shorter events, 147.9 us)
Async XLA Ops:
  7.2 227.8 %copy-start = (bf16[512,2048]{1,0:T(8,128)(2,1)S(1)}, bf16[512,2048]{1,0:T(8,128)(2,1)}, u32[]{:S(2)}) copy-start(bf16[512,2048]{1,0:T(8,128)(2,1)} %param.33) | copy-start | bytes 6291460
  7.2 139.8 %all-gather.2.cloned.1.call-start = ((), (), s32[]{:S(2)}) async-start(), calls=%async_computation.5 | async-start | bytes 1310720 | tf_op jit(solution)/shard_map/all_gather | solution.py:198
  10.3 63.3 %copy-start.16 = (s32[1024]{0:T(1024)}, s32[1024]{0:T(1024)S(1)}, u32[]{:S(2)}) copy-start(s32[1024]{0:T(1024)S(1)} %pad_clamp_fusion.1) | copy-start | bytes 12292
  12.3 61.3 %all-to-all-start.1 = ((bf16[8,4,512]{2,1,0:T(4,128)(2,1)}), bf16[8,4,512]{2,1,0:T(4,128)(2,1)S(1)}, u32[]{:S(2)}, u32[]{:S(2)}) async-start(bf16[8,4,512]{2,1,0:T(4,128)(2,1)} %reshape.354), calls=%async_computation.1 | async-start | bytes 65536 | tf_op jit(solution)/shard_map/all_to_all | solution.py:168
  17.5 46.3 %collective-permute-start = (bf16[32,4,512]{2,1,0:T(4,128)(2,1)}, bf16[32,4,512]{2,1,0:T(4,128)(2,1)S(1)}, u32[]{:S(2)}, u32[]{:S(2)}) collective-permute-start(bf16[32,4,512]{2,1,0:T(4,128)(2,1)} %param.21), channel_id=1, source_target_pairs={{0,1},{1,2},{2,3},{3,0},{4,5},{5,6},{6,7},{7,4},{8,9},{9,10},{10,1... | collective-permute-start | bytes 393224 | tf_op jit(solution)/shard_map/ppermute | solution.py:137
  63.8 28.7 %collective-permute-start.1 = (bf16[32,4,512]{2,1,0:T(4,128)(2,1)S(1)}, bf16[32,4,512]{2,1,0:T(4,128)(2,1)S(1)}, u32[]{:S(2)}, u32[]{:S(2)}) collective-permute-start(bf16[32,4,512]{2,1,0:T(4,128)(2,1)S(1)} %collective-permute-done), channel_id=1, source_target_pairs={{0,1},{1,2},{2,3},{3,0},{4,5},{5,6},{6,7},{7,4},{8,9},{9,10},{10,1... | collective-permute-start | bytes 393224 | tf_op jit(solution)/shard_map/ppermute | solution.py:137
  64.6 13.6 %copy-start.17 = (s32[1024]{0:T(1024)}, s32[1024]{0:T(1024)S(1)}, u32[]{:S(2)}) copy-start(s32[1024]{0:T(1024)S(1)} %pad_clamp_fusion) | copy-start | bytes 12292
  68.6 30.9 %copy-start.9 = (bf16[32,4,512]{2,1,0:T(4,128)(2,1)S(1)}, bf16[32,4,512]{2,1,0:T(4,128)(2,1)}, u32[]{:S(2)}) copy-start(bf16[32,4,512]{2,1,0:T(4,128)(2,1)} %param.21) | copy-start | bytes 393220
  73.6 75.7 %all-to-all-start = ((f32[8,4,8,4096]{3,2,1,0:T(8,128)}), f32[8,4,8,4096]{3,2,1,0:T(8,128)}, u32[]{:S(2)}, u32[]{:S(2)}) async-start(f32[8,4,8,4096]{3,2,1,0:T(8,128)} %bitcast.175), calls=%async_computation | async-start | bytes 8388608 | tf_op jit(solution)/shard_map/all_to_all | solution.py:167
  78.2 295.8 %reduce-scatter.3.cloned.1.call-start = ((), (), s32[]{:S(2)}) async-start(), calls=%async_computation.6 | async-start | bytes 1310720 | tf_op jit(solution)/shard_map/reduce_scatter | solution.py:236
  92.5 6.8 %collective-permute-start.2 = (bf16[32,4,512]{2,1,0:T(4,128)(2,1)S(1)}, bf16[32,4,512]{2,1,0:T(4,128)(2,1)S(1)}, u32[]{:S(2)}, u32[]{:S(2)}) collective-permute-start(bf16[32,4,512]{2,1,0:T(4,128)(2,1)S(1)} %collective-permute-done.1), channel_id=1, source_target_pairs={{0,1},{1,2},{2,3},{3,0},{4,5},{5,6},{6,7},{7,4},{8,9},{9,10},{10,1... | collective-permute-start | bytes 393224 | tf_op jit(solution)/shard_map/ppermute | solution.py:137
  93.5 18.8 %copy-start.22 = (bf16[96,512]{1,0:T(8,128)(2,1)S(1)}, bf16[96,512]{1,0:T(8,128)(2,1)}, u32[]{:S(2)}) copy-start(bf16[96,512]{1,0:T(8,128)(2,1)} %param.35) | copy-start | bytes 294916
  154.5 13.7 %copy-start.6 = (f32[32,8,64]{2,1,0:T(8,128)S(1)}, f32[32,8,64]{2,1,0:T(8,128)}, u32[]{:S(2)}) copy-start(f32[32,8,64]{2,1,0:T(8,128)} %copy.91) | copy-start | bytes 196612
  180.5 20.3 %copy-start.5 = (f32[32,8,64]{2,1,0:T(8,128)S(1)}, f32[32,8,64]{2,1,0:T(8,128)}, u32[]{:S(2)}) copy-start(f32[32,8,64]{2,1,0:T(8,128)} %copy.96) | copy-start | bytes 196612
  200.8 14.2 %copy-start.8 = (f32[32,8,64]{2,1,0:T(8,128)S(1)}, f32[32,8,64]{2,1,0:T(8,128)}, u32[]{:S(2)}) copy-start(f32[32,8,64]{2,1,0:T(8,128)} %get-tuple-element.49) | copy-start | bytes 196612
  230.7 12.7 %copy-start.19 = (pred[32,4]{0,1:T(4,128)(4,1)S(1)}, pred[32,4]{0,1:T(4,128)(4,1)}, u32[]{:S(2)}) copy-start(pred[32,4]{0,1:T(4,128)(4,1)} %get-tuple-element.84) | copy-start | bytes 388
  239.2 8.9 %all-to-all-start.2 = ((bf16[8,4,512]{2,1,0:T(4,128)(2,1)}), bf16[8,4,512]{2,1,0:T(4,128)(2,1)S(1)}, u32[]{:S(2)}, u32[]{:S(2)}) async-start(bf16[8,4,512]{2,1,0:T(4,128)(2,1)} %reshape.356), calls=%async_computation.3 | async-start | bytes 65536 | tf_op jit(solution)/shard_map/all_to_all | solution.py:169
  243.2 179.2 %reduce-scatter.5.cloned.1.call-start = ((), (), s32[]{:S(2)}) async-start(), calls=%async_computation.7 | async-start | bytes 655360 | tf_op jit(solution)/shard_map/reduce_scatter | solution.py:252
  366.0 25.3 %copy-start.12 = (f32[1,2048]{1,0:T(1,128)S(1)}, f32[1,2048]{1,0:T(1,128)}, u32[]{:S(2)}) copy-start(f32[1,2048]{1,0:T(1,128)} %get-tuple-element.62) | copy-start | bytes 24580
  375.1 23.1 %copy-start.13 = (pred[32]{0:T(512)(128)(4,1)S(1)}, pred[32]{0:T(512)(128)(4,1)}, u32[]{:S(2)}) copy-start(pred[32]{0:T(512)(128)(4,1)} %get-tuple-element.81) | copy-start | bytes 100
  375.1 23.1 %copy-start.15 = (pred[32]{0:T(512)(128)(4,1)S(1)}, pred[32]{0:T(512)(128)(4,1)}, u32[]{:S(2)}) copy-start(pred[32]{0:T(512)(128)(4,1)} %get-tuple-element.83) | copy-start | bytes 100
  375.1 23.1 %copy-start.18 = (pred[32]{0:T(512)(128)(4,1)S(1)}, pred[32]{0:T(512)(128)(4,1)}, u32[]{:S(2)}) copy-start(pred[32]{0:T(512)(128)(4,1)} %get-tuple-element.82) | copy-start | bytes 100
  375.1 23.1 %copy-start.20 = (pred[32]{0:T(512)(128)(4,1)S(1)}, pred[32]{0:T(512)(128)(4,1)}, u32[]{:S(2)}) copy-start(pred[32]{0:T(512)(128)(4,1)} %get-tuple-element.80) | copy-start | bytes 100
  398.2 26.0 %copy-start.1 = (bf16[512,2048]{1,0:T(8,128)(2,1)S(1)}, bf16[512,2048]{1,0:T(8,128)(2,1)}, u32[]{:S(2)}) copy-start(bf16[512,2048]{1,0:T(8,128)(2,1)} %param.33) | copy-start | bytes 6291460
  (8 other events, 55.2 us)
Sparse Core Ops, SparseCore 0:
  9.6 39.4 all-gather.1
  237.9 28.3 reduce-scatter.2
  398.3 19.6 reduce-scatter.4
